TPU v7x, 512 devices: a whole 4x4x16 slice. The times are simulated.
512 devices in a mesh: chan: 32 (over z_lo, y, core), day: 16 (over x, z_hi).
Axes of the slice: x: 4, y: 4, z: 16 (z_hi: 4, z_lo: 4; z = z_hi * 4 + z_lo), core: 2. Of those that a mesh axis runs over, the one named last changes fastest.
Arguments:
- records: bfloat16 [16, 2048, 4096], P('day', 'chan'), may hold values from -50 to 50
- filter_taps: bfloat16 [64], replicated, may hold values from -0.75 to 0.75
- window_offsets: int32 [16, 2], P('day'), may hold values from 0 to 3009, as said below
- pair_masks: int32 [3], replicated, may hold values from 1 to 31, as said below
Outputs:
- stacks: float32 [3, 65, 131072], P(None, None, ('chan', 'day'))
Inputs may be any that keep to these rules, and one draw needn't show every extreme that they name: `window_offsets`: in each day group one window ends at the record's last sample. `pair_masks`: the masks are distinct; 1 and 31 are among them.
All inputs are finite; a program needn't handle non-finite values.
Results may differ from a plain program's by a relative error of at most 0.0029.
Values may be sent and summed in bfloat16 or wider, within the bound.
A program may use at most 64 MiB of HBM per device.

v0:
```python
import jax
import jax.numpy as jnp
from jax import lax
from jax.sharding import PartitionSpec as P

L = 1024
MAXLAG = 32


def from_partner(value, axis, apart):
    mask = 2**apart
    pairs = [(source, source ^ mask) for source in range(lax.axis_size(axis))]
    return lax.ppermute(value, axis, pairs)


def whiten(segments, filter_taps):
    tap_count = filter_taps.shape[0]
    seg_len = segments.shape[-1]
    width = seg_len - tap_count + 1
    source_pos = jnp.arange(seg_len, dtype=jnp.int32)[:, None]
    target_pos = jnp.arange(width, dtype=jnp.int32)[None, :]
    offset = source_pos - target_pos
    inside = jnp.logical_and(offset >= 0, offset < tap_count)
    picked = jnp.take(filter_taps, jnp.clip(offset, 0, tap_count - 1))
    banded = jnp.where(inside, picked, jnp.zeros_like(picked))
    total = jnp.einsum("wcs,st->wct", segments, banded, preferred_element_type=jnp.float32)
    power = jnp.mean(total * total, axis=-1, keepdims=True)
    return (total * lax.rsqrt(power + 1e-06)).astype(jnp.bfloat16)


def correlate(mine, theirs):
    width = mine.shape[2]
    lag_count = 2 * MAXLAG + 1
    padded = jnp.pad(theirs, ((0, 0), (0, 0), (MAXLAG, MAXLAG)))
    tables = [
        jnp.einsum(
            "cwt,dwt->cd",
            mine,
            padded[:, :, lag_index : lag_index + width],
            preferred_element_type=jnp.float32,
        )
        for lag_index in range(lag_count)
    ]
    return jnp.stack(tables).reshape(lag_count, mine.shape[0] * theirs.shape[0])


def local(records, filter_taps, window_offsets, pair_masks):
    record = records[0]
    channel_count = record.shape[0]
    tap_count = filter_taps.shape[0]
    seg_len = L + tap_count - 1

    def cut_window(start):
        return lax.dynamic_slice(
            record, (jnp.zeros((), jnp.int32), start), (channel_count, seg_len)
        )

    segments = jax.vmap(cut_window)(window_offsets[0])
    white_block = jnp.transpose(whiten(segments, filter_taps), (1, 0, 2))
    rounds = pair_masks.shape[0]
    bits_count = lax.axis_size("chan").bit_length() - 1
    partners = []
    for round_index in range(rounds):
        incoming = white_block
        for bit_number in range(bits_count):
            swapped = from_partner(incoming, "chan", bit_number)
            bit_set = jnp.bitwise_and(jnp.right_shift(pair_masks[round_index], bit_number), 1) == 1
            incoming = jnp.where(bit_set, swapped, incoming)
        partners.append(incoming)
    tables = [correlate(white_block, partner_block) for partner_block in partners]
    day_total = records.shape[0] * lax.axis_size("day")
    norm_factor = 1.0 / jnp.sqrt(
        jnp.float32(day_total * window_offsets.shape[1] * white_block.shape[2])
    )
    summed_rounds = [
        lax.psum_scatter(table, "day", scatter_dimension=1, tiled=True) for table in tables
    ]
    result = jnp.stack(summed_rounds)
    return result * norm_factor


def solution(mesh):
    in_specs = (P("day", "chan", None), P(), P("day", None), P())
    out_specs = P(None, None, ("chan", "day"))
    return jax.shard_map(local, mesh=mesh, in_specs=in_specs, out_specs=out_specs, check_vma=False)
```

profile of v0, /device:TPU:24, one launch (start us, length us, event | category | flops | bytes accessed | tf_op | source)
XLA Modules:
  0.0 714.1 jit_solution(4069265529070046977)
XLA Ops:
  6.5 2.1 fusion.716
  8.6 2.1 fusion.714
  10.7 2.1 fusion.715
  15.2 4.7 while.1
  15.8 1.7 bitcast_dynamic-update-slice_fusion.2
  18.2 1.7 bitcast_dynamic-update-slice_fusion.2
  19.9 61.6 %multiply_reduce_fusion = (f32[2,64]{1,0:T(2,128)S(1)}, f32[2,64,1024]{2,1,0:T(8,128)S(1)}) fusion(bf16[2,64,1087]{2,1,0:T(8,128)(2,1)S(1)} %get-tuple-element.12, bf16[]{:T(256)} %bitcast.116, bf16[]{:T(256)} %bitcast.117, bf16[]{:T(256)} %bitcast.118, bf16[]{:T(256)} %bitcast.119, bf16[]{:T(256)} %bitcast.120, bf16[]{:T(256)} %bitcast.122, ...), kind=kOutput, calls=%fused_computation.462 | convolution fusion | flops 445497216 | bytes 803200 | tf_op jit(solution)/shard_map/wcs,st->wct/dot_general | solution.py:26
  81.5 1.9 collective-permute-start
  86.3 2.7 collective-permute-start.1
  88.9 3.2 collective-permute-start.5
  100.0 2.7 collective-permute-start.9
  102.7 8.2 %collective-permute-start.2 = (bf16[64,2,1024]{2,0,1:T(8,128)(2,1)S(1)}, bf16[64,2,1024]{2,0,1:T(8,128)(2,1)S(1)}, u32[]{:S(2)}, u32[]{:S(2)}) collective-permute-start(bf16[64,2,1024]{2,0,1:T(8,128)(2,1)S(1)} %broadcast_select_fusion.11), channel_id=1, source_target_pairs={{0,64},{16,80},{32,96},{48,112},{64,0},{80,16},{96,32},{112,48},{1... | collective-permute-start | bytes 786440 | tf_op jit(solution)/shard_map/ppermute | solution.py:13
  111.0 1.9 collective-permute-start.6
  112.9 5.4 collective-permute-start.10
  118.4 3.3 collective-permute-done.2
  121.7 1.9 collective-permute-start.3
  123.7 3.7 collective-permute-done.6
  127.3 1.9 collective-permute-start.7
  129.3 2.6 collective-permute-done.10
  131.9 1.9 collective-permute-start.11
  133.9 1.9 collective-permute-start.4
  135.9 4.8 collective-permute-start.8
  140.7 1.7 collective-permute-done.11
  142.5 2.1 collective-permute-start.12
  144.6 17.6 %collective-permute-done.4 = bf16[64,2,1024]{2,0,1:T(8,128)(2,1)S(1)} collective-permute-done((bf16[64,2,1024]{2,0,1:T(8,128)(2,1)S(1)}, bf16[64,2,1024]{2,0,1:T(8,128)(2,1)S(1)}, u32[]{:S(2)}, u32[]{:S(2)}) %collective-permute-start.4) | collective-permute-done | bytes 262176 | tf_op jit(solution)/shard_map/ppermute | solution.py:13
  346.9 14.7 %stack.671 = f32[65,4096]{1,0:T(8,128)} concatenate(f32[1,4096]{1,0:T(1,128)} %stack.606, f32[1,4096]{1,0:T(1,128)} %stack.607, f32[1,4096]{1,0:T(1,128)} %stack.608, f32[1,4096]{1,0:T(1,128)} %stack.609, f32[1,4096]{1,0:T(1,128)} %stack.610, f32[1,4096]{1,0:T(1,128)} %stack.611, f32[1,4096]{1,0:T(1,128)} %stack.612, f32[1,4096]{1,0:T(1,128)} %stack.613, f32[1,4096]{1,0:T(1,128)} %stack.614, ...), dimensions={0} | concatenate | bytes 2129920 | tf_op jit(solution)/shard_map/stack | solution.py:44
  374.6 7.4 %stack.738 = f32[65,4096]{1,0:T(8,128)} concatenate(f32[1,4096]{1,0:T(1,128)S(1)} %stack.673, f32[1,4096]{1,0:T(1,128)S(1)} %stack.674, f32[1,4096]{1,0:T(1,128)S(1)} %stack.675, f32[1,4096]{1,0:T(1,128)S(1)} %stack.676, f32[1,4096]{1,0:T(1,128)S(1)} %stack.677, f32[1,4096]{1,0:T(1,128)S(1)} %stack.678, f32[1,4096]{1,0:T(1,128)S(1)} %stack.679, f32[1,4096]{1,0:T(1,128)S(1)} %stack.680, ...), dimensions={0} | concatenate | bytes 2129920 | tf_op jit(solution)/shard_map/stack | solution.py:44
  397.9 7.4 %stack.805 = f32[65,4096]{1,0:T(8,128)} concatenate(f32[1,4096]{1,0:T(1,128)S(1)} %stack.740, f32[1,4096]{1,0:T(1,128)S(1)} %stack.741, f32[1,4096]{1,0:T(1,128)S(1)} %stack.742, f32[1,4096]{1,0:T(1,128)S(1)} %stack.743, f32[1,4096]{1,0:T(1,128)S(1)} %stack.744, f32[1,4096]{1,0:T(1,128)S(1)} %stack.745, f32[1,4096]{1,0:T(1,128)S(1)} %stack.746, f32[1,4096]{1,0:T(1,128)S(1)} %stack.747, ...), dimensions={0} | concatenate | bytes 2129920 | tf_op jit(solution)/shard_map/stack | solution.py:44
  405.3 72.1 %reduce-scatter.4.cloned.1.call-done = f32[65,256]{1,0:T(8,128)} async-done(((f32[65,4096]{1,0:T(8,128)}), f32[65,256]{1,0:T(8,128)}) %reduce-scatter.4.cloned.1.call-update) | async-done | bytes 66576 | tf_op jit(solution)/shard_map/reduce_scatter | solution.py:76
  477.4 113.9 %reduce-scatter.6.cloned.1.call-done = f32[65,256]{1,0:T(8,128)} async-done(((f32[65,4096]{1,0:T(8,128)}), f32[65,256]{1,0:T(8,128)}) %reduce-scatter.6.cloned.1.call-update) | async-done | bytes 66576 | tf_op jit(solution)/shard_map/reduce_scatter | solution.py:76
  591.3 114.4 %reduce-scatter.8.cloned.1.call-done = f32[65,256]{1,0:T(8,128)} async-done(((f32[65,4096]{1,0:T(8,128)}), f32[65,256]{1,0:T(8,128)}) %reduce-scatter.8.cloned.1.call-update) | async-done | bytes 66576 | tf_op jit(solution)/shard_map/reduce_scatter | solution.py:76
  705.7 1.7 maximum_multiply_fusion
  (441 shorter events, 216.8 us)
Async XLA Ops:
  6.5 470.8 %reduce-scatter.4.cloned.1.call-start = ((), (), s32[]{:S(2)}) async-start(), calls=%async_computation.3 | async-start | bytes 1253376 | tf_op jit(solution)/shard_map/reduce_scatter | solution.py:76
  19.9 63.6 %copy-start.5 = (s32[3]{0:T(128)S(1)}, s32[3]{0:T(128)}, u32[]{:S(2)}) copy-start(s32[3]{0:T(128)} %param.7) | copy-start | bytes 40
  81.5 4.6 collective-permute-start
  86.3 16.4 %collective-permute-start.1 = (bf16[64,2,1024]{2,0,1:T(8,128)(2,1)S(1)}, bf16[64,2,1024]{2,0,1:T(8,128)(2,1)S(1)}, u32[]{:S(2)}, u32[]{:S(2)}) collective-permute-start(bf16[64,2,1024]{2,0,1:T(8,128)(2,1)S(1)} %get-tuple-element.25), channel_id=1, source_target_pairs={{0,32},{16,48},{32,0},{48,16},{64,96},{80,112},{96,64},{112,80},{1... | collective-permute-start | bytes 786440 | tf_op jit(solution)/shard_map/ppermute | solution.py:13
  88.9 22.0 %collective-permute-start.5 = (bf16[64,2,1024]{2,0,1:T(8,128)(2,1)S(1)}, bf16[64,2,1024]{2,0,1:T(8,128)(2,1)S(1)}, u32[]{:S(2)}, u32[]{:S(2)}) collective-permute-start(bf16[64,2,1024]{2,0,1:T(8,128)(2,1)S(1)} %get-tuple-element.27), channel_id=1, source_target_pairs={{0,32},{16,48},{32,0},{48,16},{64,96},{80,112},{96,64},{112,80},{1... | collective-permute-start | bytes 786440 | tf_op jit(solution)/shard_map/ppermute | solution.py:13
  100.0 12.9 %collective-permute-start.9 = (bf16[64,2,1024]{2,0,1:T(8,128)(2,1)S(1)}, bf16[64,2,1024]{2,0,1:T(8,128)(2,1)S(1)}, u32[]{:S(2)}, u32[]{:S(2)}) collective-permute-start(bf16[64,2,1024]{2,0,1:T(8,128)(2,1)S(1)} %get-tuple-element.26), channel_id=1, source_target_pairs={{0,32},{16,48},{32,0},{48,16},{64,96},{80,112},{96,64},{112,80},{1... | collective-permute-start | bytes 786440 | tf_op jit(solution)/shard_map/ppermute | solution.py:13
  102.7 19.0 %collective-permute-start.2 = (bf16[64,2,1024]{2,0,1:T(8,128)(2,1)S(1)}, bf16[64,2,1024]{2,0,1:T(8,128)(2,1)S(1)}, u32[]{:S(2)}, u32[]{:S(2)}) collective-permute-start(bf16[64,2,1024]{2,0,1:T(8,128)(2,1)S(1)} %broadcast_select_fusion.11), channel_id=1, source_target_pairs={{0,64},{16,80},{32,96},{48,112},{64,0},{80,16},{96,32},{112,48},{1... | collective-permute-start | bytes 786440 | tf_op jit(solution)/shard_map/ppermute | solution.py:13
  111.0 16.4 %collective-permute-start.6 = (bf16[64,2,1024]{2,0,1:T(8,128)(2,1)S(1)}, bf16[64,2,1024]{2,0,1:T(8,128)(2,1)S(1)}, u32[]{:S(2)}, u32[]{:S(2)}) collective-permute-start(bf16[64,2,1024]{2,0,1:T(8,128)(2,1)S(1)} %broadcast_select_fusion.6), channel_id=1, source_target_pairs={{0,64},{16,80},{32,96},{48,112},{64,0},{80,16},{96,32},{112,48},{1... | collective-permute-start | bytes 786440 | tf_op jit(solution)/shard_map/ppermute | solution.py:13
  112.9 19.0 %collective-permute-start.10 = (bf16[64,2,1024]{2,0,1:T(8,128)(2,1)S(1)}, bf16[64,2,1024]{2,0,1:T(8,128)(2,1)S(1)}, u32[]{:S(2)}, u32[]{:S(2)}) collective-permute-start(bf16[64,2,1024]{2,0,1:T(8,128)(2,1)S(1)} %broadcast_select_fusion.1), channel_id=1, source_target_pairs={{0,64},{16,80},{32,96},{48,112},{64,0},{80,16},{96,32},{112,48},{1... | collective-permute-start | bytes 786440 | tf_op jit(solution)/shard_map/ppermute | solution.py:13
  121.7 12.1 %collective-permute-start.3 = (bf16[64,2,1024]{2,0,1:T(8,128)(2,1)S(1)}, bf16[64,2,1024]{2,0,1:T(8,128)(2,1)S(1)}, u32[]{:S(2)}, u32[]{:S(2)}) collective-permute-start(bf16[64,2,1024]{2,0,1:T(8,128)(2,1)S(1)} %broadcast_select_fusion.12), channel_id=1, source_target_pairs={{0,128},{16,144},{32,160},{48,176},{64,192},{80,208},{96,224},{112... | collective-permute-start | bytes 786440 | tf_op jit(solution)/shard_map/ppermute | solution.py:13
  127.3 8.5 %collective-permute-start.7 = (bf16[64,2,1024]{2,0,1:T(8,128)(2,1)S(1)}, bf16[64,2,1024]{2,0,1:T(8,128)(2,1)S(1)}, u32[]{:S(2)}, u32[]{:S(2)}) collective-permute-start(bf16[64,2,1024]{2,0,1:T(8,128)(2,1)S(1)} %broadcast_select_fusion.7), channel_id=1, source_target_pairs={{0,128},{16,144},{32,160},{48,176},{64,192},{80,208},{96,224},{112... | collective-permute-start | bytes 786440 | tf_op jit(solution)/shard_map/ppermute | solution.py:13
  131.9 10.5 %collective-permute-start.11 = (bf16[64,2,1024]{2,0,1:T(8,128)(2,1)S(1)}, bf16[64,2,1024]{2,0,1:T(8,128)(2,1)S(1)}, u32[]{:S(2)}, u32[]{:S(2)}) collective-permute-start(bf16[64,2,1024]{2,0,1:T(8,128)(2,1)S(1)} %broadcast_select_fusion.2), channel_id=1, source_target_pairs={{0,128},{16,144},{32,160},{48,176},{64,192},{80,208},{96,224},{112... | collective-permute-start | bytes 786440 | tf_op jit(solution)/shard_map/ppermute | solution.py:13
  133.9 28.3 %collective-permute-start.4 = (bf16[64,2,1024]{2,0,1:T(8,128)(2,1)S(1)}, bf16[64,2,1024]{2,0,1:T(8,128)(2,1)S(1)}, u32[]{:S(2)}, u32[]{:S(2)}) collective-permute-start(bf16[64,2,1024]{2,0,1:T(8,128)(2,1)S(1)} %broadcast_select_fusion.13), channel_id=1, source_target_pairs={{0,256},{16,272},{32,288},{48,304},{64,320},{80,336},{96,352},{112... | collective-permute-start | bytes 786440 | tf_op jit(solution)/shard_map/ppermute | solution.py:13
  135.9 85.4 %collective-permute-start.8 = (bf16[64,2,1024]{2,0,1:T(8,128)(2,1)S(1)}, bf16[64,2,1024]{2,0,1:T(8,128)(2,1)S(1)}, u32[]{:S(2)}, u32[]{:S(2)}) collective-permute-start(bf16[64,2,1024]{2,0,1:T(8,128)(2,1)S(1)} %broadcast_select_fusion.8), channel_id=1, source_target_pairs={{0,256},{16,272},{32,288},{48,304},{64,320},{80,336},{96,352},{112... | collective-permute-start | bytes 786440 | tf_op jit(solution)/shard_map/ppermute | solution.py:13
  142.5 101.3 %collective-permute-start.12 = (bf16[64,2,1024]{2,0,1:T(8,128)(2,1)S(1)}, bf16[64,2,1024]{2,0,1:T(8,128)(2,1)S(1)}, u32[]{:S(2)}, u32[]{:S(2)}) collective-permute-start(bf16[64,2,1024]{2,0,1:T(8,128)(2,1)S(1)} %broadcast_select_fusion.3), channel_id=1, source_target_pairs={{0,256},{16,272},{32,288},{48,304},{64,320},{80,336},{96,352},{112... | collective-permute-start | bytes 786440 | tf_op jit(solution)/shard_map/ppermute | solution.py:13
  361.7 229.6 %reduce-scatter.6.cloned.1.call-start = ((), (), s32[]{:S(2)}) async-start(), calls=%async_computation.4 | async-start | bytes 1253376 | tf_op jit(solution)/shard_map/reduce_scatter | solution.py:76
  370.2 4.4 copy-start
  370.2 4.4 copy-start.1
  370.2 4.4 copy-start.2
  370.2 4.4 copy-start.3
  370.2 4.4 copy-start.4
  386.7 319.0 %reduce-scatter.8.cloned.1.call-start = ((), (), s32[]{:S(2)}) async-start(), calls=%async_computation.5 | async-start | bytes 1253376 | tf_op jit(solution)/shard_map/reduce_scatter | solution.py:76
Sparse Core Ops, SparseCore 0:
  361.8 115.5 reduce-scatter.3
  481.5 109.8 reduce-scatter.5
  595.4 110.2 reduce-scatter.7
where the time goes:
time: 727 us; the launch traced here: 714 us
  waiting for transfers between devices  329 us (45%)
  matrix products  162 us (22%)
  local copies, waits for them, and re-layouts  154 us (21%)
  starting transfers between devices  41 us (6%)
  between operations  25.1 us (3%)
    reduce_scatter x3, waiting for transfers between devices, local(): lax.psum_scatter(table, 'day', scatter_dimension=1, tiled=True)  300 us
    another operation x198, local copies, waits for them, and re-layouts, correlate(): return jnp.stack(tables).reshape(lag_count, mine.shape[0] * theirs.shape[0])  140 us
    dot_general x195, matrix products, correlate(): jnp.einsum('cwt,dwt->cd', mine, padded[:, :, lag_index:lag_index + width]...  100 us
    dot_general x1, matrix products, whiten(): jnp.einsum('wcs,st->wct', segments, banded, preferred_element_type=jnp.fl...  61.6 us
    ppermute x13, starting transfers between devices, from_partner(): return lax.ppermute(value, axis, pairs)  40.6 us
    ppermute x13, waiting for transfers between devices, from_partner(): return lax.ppermute(value, axis, pairs)  29 us
  transfers between devices with their start and end apart: 16, of which 8 were waited for; matrix products, arithmetic and copies ran while one was open for 17% of the time, Pallas kernels for 0%

commit v1 on v0

v1 whole, which is shorter than its diff:
```python
import functools

import jax
import jax.numpy as jnp
from jax import lax
from jax.experimental import pallas as pl
from jax.experimental.pallas import tpu as pltpu
from jax.sharding import PartitionSpec as P

MESH = pl.DeviceIdType.MESH
F32, BF16 = jnp.float32, jnp.bfloat16
NT = (((1,), (1,)), ((), ()))

L, MAXLAG, TAPS = 1024, 32, 64
LAGS = 2 * MAXLAG + 1
CH = 64
STEP = 16
DELAYS = STEP + 1
GAP = 128
ROW = 2 * (L + GAP)
RING = 4
XR = DELAYS * STEP
XH = 144
ZR = 80
ZH = 48


def whiten_kernel(offsets, record, taps, white, band):
    width = 384
    band[...] = jnp.zeros_like(band)
    band[0:1, 0:TAPS] = taps[...].astype(F32)
    rows = jnp.broadcast_to(band[0:1, :], (256, width))
    toeplitz = pltpu.roll(rows, 0, 1, stride=1, stride_axis=0).astype(BF16)
    span = 1280
    last = (record.shape[1] - span) // 128
    for w in range(2):
        start = offsets[0, w]
        tile = jnp.minimum(start // 128, last)
        base = pl.multiple_of(tile * 128, 128)
        data = record[:, pl.ds(base, span)].astype(F32)
        data = pltpu.roll(data, span - (start - base), 1).astype(BF16)
        parts = jnp.concatenate([data[:, 256 * m : 256 * m + width] for m in range(4)], axis=0)
        total = lax.dot_general(parts, toeplitz, NT, preferred_element_type=F32)
        square = jnp.sum(total * total, axis=1, keepdims=True)
        power = sum(square[CH * m : CH * (m + 1)] for m in range(4)) / L
        scale = lax.rsqrt(power + 1e-06)
        for m in range(4):
            lanes = slice(L * w + 256 * m, L * w + 256 * (m + 1))
            white[:, lanes] = (total[CH * m : CH * (m + 1)] * scale).astype(BF16)


def gapped(block):
    zeros = jnp.zeros((CH, GAP), BF16)
    return jnp.concatenate([block[:, :L], zeros, block[:, L:], zeros], axis=1)


class Ring:
    def __init__(self, half, right, left, far, near_r, near_l, hop_r, hop_l, got_l, got_r, send, recv):
        self.half = half
        self.right, self.left = right, left
        self.far, self.near_r, self.near_l = far, near_r, near_l
        self.hop_r, self.hop_l, self.got_l, self.got_r = hop_r, hop_l, got_l, got_r
        self.send, self.recv = send, recv

    def copy(self, r, k):
        lo, hi = pl.ds(0, self.half), pl.ds(self.half, self.far.shape[1] - self.half)
        src, dst, to = (
            (self.far.at[r, lo], self.hop_r.at[r], self.right),
            (self.far.at[r, hi], self.hop_l.at[r], self.left),
            (self.near_r.at[r, hi], self.got_l.at[r, hi], self.right),
            (self.near_l.at[r, lo], self.got_r.at[r, lo], self.left),
            (self.near_r.at[r, lo], self.got_l.at[r, lo], self.right),
            (self.near_l.at[r, hi], self.got_r.at[r, hi], self.left),
        )[k]
        return pltpu.make_async_remote_copy(
            src_ref=src, dst_ref=dst, send_sem=self.send.at[r, k], recv_sem=self.recv.at[r, k],
            device_id={"day": to}, device_id_type=MESH,
        )


def reduce_kernel(
    own, p0, p1, p2, out,
    astack, bstack, c_own, c_r, c_l, s_buf, z_buf,
    x_far, x_r, x_l, x_hr, x_hl, x_gl, x_gr, xs, xd,
    z_far, z_r, z_l, z_hr, z_hl, z_gl, z_gr, zs, zd,
):
    day = lax.axis_index("day")
    x, zh = day // RING, day % RING
    x_right, x_left = ((x + 1) % RING) * RING + zh, ((x + 3) % RING) * RING + zh
    z_right, z_left = x * RING + (zh + 1) % RING, x * RING + (zh + 3) % RING
    barrier = pltpu.get_barrier_semaphore()
    for other in (x_right, x_left, z_right, z_left):
        pl.semaphore_signal(barrier, inc=1, device_id={"day": other}, device_id_type=MESH)

    xring = Ring(XH, x_right, x_left, x_far, x_r, x_l, x_hr, x_hl, x_gl, x_gr, xs, xd)
    zring = Ring(ZH, z_right, z_left, z_far, z_r, z_l, z_hr, z_hl, z_gl, z_gr, zs, zd)

    mine = gapped(own[...])
    for a in range(DELAYS):
        moved = pltpu.roll(mine, a, 1) if a else mine
        for part in range(RING):
            astack[part, 16 * a : 16 * a + 16, :] = moved[16 * part : 16 * part + 16]
    pl.semaphore_wait(barrier, 4)

    norm = 1.0 / jnp.sqrt(jnp.float32(16 * 2 * L))

    def product(part):
        return lax.dot_general(astack[part], bstack[...], NT, preferred_element_type=F32)

    def compute(r):
        theirs = gapped((p0, p1, p2)[r][...])
        for b in range(4):
            shift = (MAXLAG - STEP * b) % ROW
            bstack[CH * b : CH * (b + 1), :] = pltpu.roll(theirs, shift, 1) if shift else theirs
        x_far[r] = product((x + 2) % RING).astype(BF16)
        xring.copy(r, 0).start()
        xring.copy(r, 1).start()
        piece = product((x + 1) % RING)
        x_r[r, XH:, :] = piece[XH:].astype(BF16)
        xring.copy(r, 2).start()
        c_r[r] = piece[:XH]
        piece = product((x + 3) % RING)
        x_l[r, :XH, :] = piece[:XH].astype(BF16)
        xring.copy(r, 3).start()
        c_l[r] = piece[XH:]
        c_own[r] = product(x)

    def x_merge(r):
        xring.copy(r, 0).wait_recv()
        x_r[r, :XH, :] = (c_r[r] + x_hr[r].astype(F32)).astype(BF16)
        xring.copy(r, 4).start()
        xring.copy(r, 1).wait_recv()
        x_l[r, XH:, :] = (c_l[r] + x_hl[r].astype(F32)).astype(BF16)
        xring.copy(r, 5).start()

    def x_end(r):
        for k in (2, 3, 4, 5):
            xring.copy(r, k).wait_recv()
        total = c_own[r] + x_gl[r].astype(F32) + x_gr[r].astype(F32)
        for h in range(2):
            s_buf[h] = total[:, 128 * h : 128 * (h + 1)]
        for part in range(RING):
            for i in range(4):
                for h in range(2):
                    z_buf[r, part, 16 * i : 16 * i + 16, 128 * h : 128 * (h + 1)] = s_buf[
                        h, pl.ds(4 * part + i, 16, stride=16), :
                    ]
            z_buf[r, part, 64:80, :] = total[256:272]
        z_far[r] = z_buf[r, (zh + 2) % RING].astype(BF16)
        zring.copy(r, 0).start()
        zring.copy(r, 1).start()
        z_r[r, ZH:, :] = z_buf[r, (zh + 1) % RING, ZH:, :].astype(BF16)
        zring.copy(r, 2).start()
        z_l[r, :ZH, :] = z_buf[r, (zh + 3) % RING, :ZH, :].astype(BF16)
        zring.copy(r, 3).start()

    def z_merge(r):
        zring.copy(r, 0).wait_recv()
        z_r[r, :ZH, :] = (z_buf[r, (zh + 1) % RING, :ZH, :] + z_hr[r].astype(F32)).astype(BF16)
        zring.copy(r, 4).start()
        zring.copy(r, 1).wait_recv()
        z_l[r, ZH:, :] = (z_buf[r, (zh + 3) % RING, ZH:, :] + z_hl[r].astype(F32)).astype(BF16)
        zring.copy(r, 5).start()

    def z_end(r):
        for k in (2, 3, 4, 5):
            zring.copy(r, k).wait_recv()
        total = (z_buf[r, zh] + z_gl[r].astype(F32) + z_gr[r].astype(F32)) * norm
        for b in range(4):
            cut = total[:64, CH * b : CH * (b + 1)]
            for pair in range(2):
                out[r, 16 * b : 16 * b + 16, 128 * pair : 128 * (pair + 1)] = jnp.concatenate(
                    [cut[32 * pair : 32 * pair + 16], cut[32 * pair + 16 : 32 * pair + 32]], axis=1
                )
        tail = total[64:68, 192:256]
        for part in range(1, RING):
            tail = jnp.where(zh == part, total[64 + 4 * part : 68 + 4 * part, 192:256], tail)
        out[r, 64:65, :] = jnp.concatenate([tail[i : i + 1] for i in range(4)], axis=1)

    compute(0)
    compute(1)
    x_merge(0)
    compute(2)
    x_end(0)
    x_merge(1)
    z_merge(0)
    x_end(1)
    x_merge(2)
    z_merge(1)
    x_end(2)
    z_end(0)
    z_merge(2)
    z_end(1)
    z_end(2)
    for r in range(3):
        for k in range(6):
            xring.copy(r, k).wait_send()
            zring.copy(r, k).wait_send()


def ring_scratch(rows, half):
    full = pltpu.VMEM((3, rows, 256), BF16)
    return [
        full, full, full,
        pltpu.VMEM((3, half, 256), BF16), pltpu.VMEM((3, rows - half, 256), BF16),
        full, full,
        pltpu.SemaphoreType.DMA((3, 6)), pltpu.SemaphoreType.DMA((3, 6)),
    ]


def partner(value, mask):
    count = lax.axis_size("chan")
    return lax.ppermute(value, "chan", [(i, i ^ mask) for i in range(count)])


def local(records, filter_taps, window_offsets, pair_masks):
    vmem = pl.BlockSpec(memory_space=pltpu.VMEM)
    white = pl.pallas_call(
        whiten_kernel,
        out_shape=jax.ShapeDtypeStruct((CH, 2 * L), BF16),
        in_specs=[pl.BlockSpec(memory_space=pltpu.SMEM), vmem, vmem],
        out_specs=vmem,
        scratch_shapes=[pltpu.VMEM((8, 384), F32)],
        compiler_params=pltpu.CompilerParams(vmem_limit_bytes=16 << 20),
        name="whiten",
    )(window_offsets, records[0], filter_taps[None])

    count = lax.axis_size("chan")
    middle = jnp.sum(pair_masks) - count
    near = partner(white, 1)
    far = partner(white, count - 1)
    other = lax.switch(middle - 2, [functools.partial(partner, mask=m) for m in range(2, count - 1)], white)

    res = pl.pallas_call(
        reduce_kernel,
        out_shape=jax.ShapeDtypeStruct((3, LAGS, 256), F32),
        in_specs=[vmem] * 4,
        out_specs=vmem,
        scratch_shapes=[
            pltpu.VMEM((RING, XR, ROW), BF16),
            pltpu.VMEM((4 * CH, ROW), BF16),
            pltpu.VMEM((3, XR, 256), F32),
            pltpu.VMEM((3, XH, 256), F32),
            pltpu.VMEM((3, XR - XH, 256), F32),
            pltpu.VMEM((2, XR, 128), F32),
            pltpu.VMEM((3, RING, ZR, 256), F32),
            *ring_scratch(XR, XH),
            *ring_scratch(ZR, ZH),
        ],
        compiler_params=pltpu.CompilerParams(collective_id=0, has_side_effects=True, vmem_limit_bytes=48 << 20),
        name="correlate",
    )(white, near, far, other)
    kind = pair_masks[:, None, None]
    return jnp.where(kind == 1, res[0], jnp.where(kind == count - 1, res[1], res[2]))


def solution(mesh):
    in_specs = (P("day", "chan", None), P(), P("day", None), P())
    out_specs = P(None, None, ("chan", "day"))
    return jax.shard_map(local, mesh=mesh, in_specs=in_specs, out_specs=out_specs, check_vma=False)
```

time: 727 us -> 81.9 us (0.11)
  the two profiles are of different devices: /device:TPU:24 before, /device:TPU:80 now
where the time goes in v1:
time: 81.9 us; the launch traced here: 81.6 us
  Pallas kernels  49.4 us (60%)
  waiting for transfers between devices  18.6 us (23%)
  starting transfers between devices  9.71 us (12%)
  local copies, waits for them, and re-layouts  1.73 us (2%)
  other arithmetic  1.42 us (2%)
    pallas_call x1, Pallas kernels, local(): pl.pallas_call(reduce_kernel, out_shape=jax.ShapeDtypeStruct((3, LAGS, 25...  48.3 us
    ppermute x3, waiting for transfers between devices, partner(): return lax.ppermute(value, 'chan', [(i, i ^ mask) for i in range(count)])  18.6 us
    ppermute x3, starting transfers between devices, partner(): return lax.ppermute(value, 'chan', [(i, i ^ mask) for i in range(count)])  9.71 us
    unnamed x8, local copies, waits for them, and re-layouts  1.71 us
  transfers between devices with their start and end apart: 3, of which 1 were waited for; matrix products, arithmetic and copies ran while one was open for 1% of the time, Pallas kernels for 0%

profile of v1, /device:TPU:80, one launch (start us, length us, event | category | flops | bytes accessed | tf_op | source)
XLA Modules:
  0.0 81.6 jit_solution(14800493807753759563)
XLA Ops:
  0.0 0.0 copy-start.1
  0.0 0.0 copy-start.2
  0.0 0.7 copy-done.1
  0.7 0.0 copy-done.2
  0.7 0.0 copy-start
  0.7 1.0 %copy-done = bf16[1,64,4096]{2,1,0:T(8,128)(2,1)S(1)} copy-done((bf16[1,64,4096]{2,1,0:T(8,128)(2,1)S(1)}, bf16[1,64,4096]{2,1,0:T(8,128)(2,1)}, u32[]{:S(2)}) %copy-start) | copy-done | bytes 524312
  1.7 0.0 copy-start.3
  1.7 1.1 %whiten.1.own = bf16[64,2048]{1,0:T(8,128)(2,1)S(1)} custom-call(s32[1,2]{1,0:T(1,128)S(1)} %copy-done.1, bf16[64,4096]{1,0:T(8,128)(2,1)S(1)} %bitcast.8, bf16[1,64]{1,0:T(2,128)(2,1)S(1)} %bitcast.9), custom_call_target="tpu_custom_call" | custom-call | tf_op jit(solution)/shard_map/whiten/pallas_call | solution.py:218
  2.8 1.9 %collective-permute-start.30 = (bf16[64,2048]{1,0:T(8,128)(2,1)S(1)}, bf16[64,2048]{1,0:T(8,128)(2,1)S(1)}, u32[]{:S(2)}, u32[]{:S(2)}) collective-permute-start(bf16[64,2048]{1,0:T(8,128)(2,1)S(1)} %whiten.1.own), channel_id=1, source_target_pairs={{0,496},{16,480},{32,464},{48,448},{64,432},{80,416},{96,400},{112... | collective-permute-start | bytes 786440 | tf_op jit(solution)/shard_map/ppermute | solution.py:213
  4.8 2.0 %collective-permute-start.29 = (bf16[64,2048]{1,0:T(8,128)(2,1)S(1)}, bf16[64,2048]{1,0:T(8,128)(2,1)S(1)}, u32[]{:S(2)}, u32[]{:S(2)}) collective-permute-start(bf16[64,2048]{1,0:T(8,128)(2,1)S(1)} %whiten.1.own), channel_id=1, source_target_pairs={{0,16},{16,0},{32,48},{48,32},{64,80},{80,64},{96,112},{112,96},{1... | collective-permute-start | bytes 786440 | tf_op jit(solution)/shard_map/ppermute | solution.py:213
  6.8 0.0 copy-done.3
  6.8 0.6 reduce_sum.9
  8.1 24.4 %conditional.1 = (bf16[64,2048]{1,0:T(8,128)(2,1)}) conditional(s32[]{:T(128)} %clamp.3, bf16[64,2048]{1,0:T(8,128)(2,1)S(1)} %whiten.1.own, bf16[64,2048]{1,0:T(8,128)(2,1)S(1)} %whiten.1.own, bf16[64,2048]{1,0:T(8,128)(2,1)S(1)} %whiten.1.own, bf16[64,2048]{1,0:T(8,128)(2,1)S(1)} %whiten.1.own, ...), branch_computations={%region_1.0_spmd, %region_2.0_spmd, %region_3.0_spmd, %region_4.0_... | conditional | bytes 1048624 | solution.py:232
  8.1 5.8 %collective-permute-start.27 = (bf16[64,2048]{1,0:T(8,128)(2,1)S(1)}, bf16[64,2048]{1,0:T(8,128)(2,1)}, u32[]{:S(2)}, u32[]{:S(2)}) collective-permute-start(bf16[64,2048]{1,0:T(8,128)(2,1)S(1)} %param.27), channel_id=1, source_target_pairs={{0,464},{16,448},{32,496},{48,480},{64,400},{80,384},{96,432},{112... | collective-permute-start | bytes 786440 | tf_op jit(solution)/shard_map/cond/branch_27_fun/ppermute | solution.py:213
  13.9 18.6 %collective-permute-done.27 = bf16[64,2048]{1,0:T(8,128)(2,1)} collective-permute-done((bf16[64,2048]{1,0:T(8,128)(2,1)S(1)}, bf16[64,2048]{1,0:T(8,128)(2,1)}, u32[]{:S(2)}, u32[]{:S(2)}) %collective-permute-start.27) | collective-permute-done | bytes 262176 | tf_op jit(solution)/shard_map/cond/branch_27_fun/ppermute | solution.py:213
  32.5 0.0 collective-permute-done.30.p1
  32.5 0.0 collective-permute-done.29.p0
  32.5 48.3 %correlate.1 = f32[3,65,256]{2,1,0:T(8,128)S(1)} custom-call(bf16[64,2048]{1,0:T(8,128)(2,1)S(1)} %whiten.1.own, bf16[64,2048]{1,0:T(8,128)(2,1)S(1)} %collective-permute-done.29.p0, bf16[64,2048]{1,0:T(8,128)(2,1)S(1)} %collective-permute-done.30.p1, bf16[64,2048]{1,0:T(8,128)(2,1)} %get-tuple-element.69.p2), custom_call_target="tpu_custom_call" | custom-call | tf_op jit(solution)/shard_map/correlate/pallas_call | solution.py:234
  80.8 0.8 select_select_fusion
  (2 shorter events, 0.0 us)
Async XLA Ops:
  0.0 0.7 copy-start.1
  0.0 0.7 copy-start.2
  0.7 1.0 %copy-start = (bf16[1,64,4096]{2,1,0:T(8,128)(2,1)S(1)}, bf16[1,64,4096]{2,1,0:T(8,128)(2,1)}, u32[]{:S(2)}) copy-start(bf16[1,64,4096]{2,1,0:T(8,128)(2,1)} %param.33) | copy-start | bytes 1572868
  1.7 5.1 %copy-start.3 = (s32[3]{0:T(128)S(1)}, s32[3]{0:T(128)}, u32[]{:S(2)}) copy-start(s32[3]{0:T(128)} %param.36) | copy-start | bytes 40
  2.8 29.7 %collective-permute-start.30 = (bf16[64,2048]{1,0:T(8,128)(2,1)S(1)}, bf16[64,2048]{1,0:T(8,128)(2,1)S(1)}, u32[]{:S(2)}, u32[]{:S(2)}) collective-permute-start(bf16[64,2048]{1,0:T(8,128)(2,1)S(1)} %whiten.1.own), channel_id=1, source_target_pairs={{0,496},{16,480},{32,464},{48,448},{64,432},{80,416},{96,400},{112... | collective-permute-start | bytes 786440 | tf_op jit(solution)/shard_map/ppermute | solution.py:213
  4.8 27.8 %collective-permute-start.29 = (bf16[64,2048]{1,0:T(8,128)(2,1)S(1)}, bf16[64,2048]{1,0:T(8,128)(2,1)S(1)}, u32[]{:S(2)}, u32[]{:S(2)}) collective-permute-start(bf16[64,2048]{1,0:T(8,128)(2,1)S(1)} %whiten.1.own), channel_id=1, source_target_pairs={{0,16},{16,0},{32,48},{48,32},{64,80},{80,64},{96,112},{112,96},{1... | collective-permute-start | bytes 786440 | tf_op jit(solution)/shard_map/ppermute | solution.py:213
  8.1 24.4 %collective-permute-start.27 = (bf16[64,2048]{1,0:T(8,128)(2,1)S(1)}, bf16[64,2048]{1,0:T(8,128)(2,1)}, u32[]{:S(2)}, u32[]{:S(2)}) collective-permute-start(bf16[64,2048]{1,0:T(8,128)(2,1)S(1)} %param.27), channel_id=1, source_target_pairs={{0,464},{16,448},{32,496},{48,480},{64,400},{80,384},{96,432},{112... | collective-permute-start | bytes 786440 | tf_op jit(solution)/shard_map/cond/branch_27_fun/ppermute | solution.py:213
